TPU v7x, 256 devices: a whole 4x4x8 slice. The times are simulated.
256 devices in a mesh: front: 4 (over y), pivot: 8 (over x, core), rows: 8 (over z).
Axes of the slice: x: 4, y: 4, z: 8, core: 2. Of those that a mesh axis runs over, the one named last changes fastest.
Arguments:
- factor: float32 [4, 8, 1024, 8192], P('front', 'pivot', 'rows'), may hold values from -0.0625 to 0.0625
- inv_diag: float32 [4, 8, 1024, 1024], P('front', 'pivot', 'rows'), may hold values from -0.1875 to 0.1875
- boundary: float32 [4, 8192, 8192], P('front', ('pivot', 'rows')), may hold values from -0.0625 to 0.0625
- rhs: float32 [4, 240, 8192], P('front', None, ('pivot', 'rows')), may hold values from -6 to 6
- boundary_rhs: float32 [4, 240, 8192], P('front', None, ('pivot', 'rows')), may hold values from -6 to 6
- owner: int32 [4, 8192, 1], P('front', ('pivot', 'rows')), may hold values from 0 to 63; in each aligned block of 128 rows (0 to 127, 128 to 255, ..., all dimensions but the last counted through in order) at most 4 rows name the same one
- slot: int32 [4, 8192], P('front', ('pivot', 'rows')), may hold values from 0 to 255
- parent_in: float32 [240, 16384], P(None, ('pivot', 'rows')), may hold values from -6 to 6
Outputs:
- solution: float32 [4, 240, 8192], P('front', None, ('pivot', 'rows'))
- parent_rhs: float32 [240, 16384], P(None, ('pivot', 'rows'))
Inputs may be any that keep to these rules, and one draw needn't show every extreme that they name: Within the 128 boundary rows of one device no owner is named more than 4 times, and in every draw some device's rows name some owner exactly 4 times.
All inputs are finite; a program needn't handle non-finite values.
Results may differ from a plain program's by a relative error of at most 0.0001.
Values sent between devices are 32-bit elements; how exact they have to be, the bound alone decides.
A program may use at most 64 MiB of HBM per device.

v0:
```python
import jax
import jax.numpy as jnp
from jax import lax
from jax.sharding import PartitionSpec as P

highest = lax.Precision.HIGHEST


def shards(factor, inv_diag, boundary, rhs, boundary_rhs, owner, slot, parent_in):
    factor_rows = factor[0, 0]
    inv_rows = inv_diag[0, 0]
    bound_rows = boundary[0]
    local_rhs = rhs[0]
    local_brhs = boundary_rhs[0]
    block_count = lax.axis_size("pivot")
    row_count = lax.axis_size("rows")
    block_span = inv_rows.shape[1]
    slice_rows = factor_rows.shape[0]
    sources = local_rhs.shape[0]
    own_block = lax.axis_index("pivot")
    own_row = lax.axis_index("rows")
    contract = (((1,), (1,)), ((), ()))

    def solve_section(section_idx, carry):
        running, boundary_sum, own_solved = carry
        residual = local_rhs - running
        partial_value = jnp.dot(
            residual, inv_rows, precision=highest, preferred_element_type=jnp.float32
        )
        masked = jnp.where(own_block == section_idx, partial_value, 0.0)
        solved = lax.psum(masked, ("pivot", "rows"))
        pivot_tile = lax.dynamic_slice_in_dim(factor_rows, section_idx * block_span, block_span, 1)
        update_term = lax.dot_general(
            solved, pivot_tile, contract, precision=highest, preferred_element_type=jnp.float32
        )
        running = running + jnp.where(section_idx < own_block, update_term, 0.0)
        bound_tile = lax.dynamic_slice_in_dim(bound_rows, section_idx * block_span, block_span, 1)
        boundary_sum = boundary_sum + lax.dot_general(
            solved, bound_tile, contract, precision=highest, preferred_element_type=jnp.float32
        )
        own_piece = lax.dynamic_slice_in_dim(solved, own_row * slice_rows, slice_rows, 1)
        own_solved = jnp.where(own_block == section_idx, own_piece, own_solved)
        return (running, boundary_sum, own_solved)

    start = (
        jnp.zeros((sources, slice_rows), jnp.float32),
        jnp.zeros((sources, bound_rows.shape[0]), jnp.float32),
        jnp.zeros((sources, slice_rows), jnp.float32),
    )
    running, boundary_sum, own_solved = lax.fori_loop(0, block_count, solve_section, start)
    update = local_brhs - boundary_sum
    out_rows = update.T
    owners = owner[0, :, 0]
    slot_ids = slot[0]
    owner_count = block_count * row_count
    capacity = max(2, 2 * out_rows.shape[0] // owner_count)
    onehot = (owners[:, None] == jnp.arange(owner_count, dtype=jnp.int32)[None, :]).astype(
        jnp.int32
    )
    before = jnp.cumsum(onehot, axis=0) - onehot
    position = jnp.sum(before * onehot, axis=1)
    dest_slot = owners * capacity + position
    select = dest_slot[None, :] == jnp.arange(owner_count * capacity, dtype=jnp.int32)[:, None]
    send_rows = jnp.dot(
        select.astype(jnp.float32), out_rows, precision=highest, preferred_element_type=jnp.float32
    )
    send_slot = jnp.max(jnp.where(select, slot_ids[None, :], -1), axis=1)
    got_rows, got_slots = (
        lax.all_to_all(
            send_rows.reshape(owner_count, capacity, sources),
            ("pivot", "rows"),
            split_axis=0,
            concat_axis=0,
            tiled=True,
        ),
        lax.all_to_all(
            send_slot.reshape(owner_count, capacity),
            ("pivot", "rows"),
            split_axis=0,
            concat_axis=0,
            tiled=True,
        ),
    )
    got_rows = got_rows.reshape(owner_count * capacity, sources)
    got_slots = got_slots.reshape(owner_count * capacity)
    parent_rows = parent_in.shape[1]
    slot_hits = (got_slots[:, None] == jnp.arange(parent_rows, dtype=jnp.int32)[None, :]).astype(
        jnp.float32
    )
    local_part = jnp.einsum(
        "ks,ko->so", got_rows, slot_hits, precision=highest, preferred_element_type=jnp.float32
    )
    sibling_total = lax.psum(local_part, "front")
    parent = parent_in + sibling_total
    return (own_solved[None], parent)


def solution(mesh):
    placed = (
        P("front", "pivot", "rows", None),
        P("front", "pivot", "rows", None),
        P("front", ("pivot", "rows"), None),
        P("front", None, ("pivot", "rows")),
        P("front", None, ("pivot", "rows")),
        P("front", ("pivot", "rows"), None),
        P("front", ("pivot", "rows")),
        P(None, ("pivot", "rows")),
    )
    return jax.shard_map(
        shards,
        mesh=mesh,
        in_specs=placed,
        out_specs=(P("front", None, ("pivot", "rows")), P(None, ("pivot", "rows"))),
        check_vma=False,
    )
```

profile of v0, /device:TPU:2, one launch (start us, length us, event | category | flops | bytes accessed | tf_op | source)
XLA Modules:
  0.0 1667.7 jit_solution(10472206007967670768)
XLA Ops:
  11.9 12.0 all-to-all-start.1
  24.0 1568.2 %while.20 = (s32[]{:T(128)}, f32[240,128]{1,0:T(8,128)S(1)}, f32[240,128]{1,0:T(8,128)S(1)}, f32[240,128]{1,0:T(8,128)S(1)}, s32[]{:T(128)}, /*index=5*/f32[240,...) while((s32[]{:T(128)}, f32[240,128]{1,0:T(8,128)S(1)}, ...), condition=%wide.region_2.3_spmd.clone, body=%wide.region_0.2_spmd.clone.sunk | while | flops 1133230080 | bytes 11526409 | solution.py:50
  24.1 3.1 convolution_select_fusion.3
  27.2 189.0 %all-reduce.5.cloned.1.call-done = f32[240,1024]{1,0:T(8,128)} async-done(((f32[240,1024]{1,0:T(8,128)}), f32[240,1024]{1,0:T(8,128)}) %all-reduce.5.cloned.1.call-update) | async-done | bytes 983056 | tf_op jit(solution)/shard_map/while/body/eval_jaxpr/psum | solution.py:31
  216.2 2.3 convolution_add_fusion.2
  221.9 3.0 convolution_select_fusion.3
  224.9 187.0 %all-reduce.5.cloned.1.call-done = f32[240,1024]{1,0:T(8,128)} async-done(((f32[240,1024]{1,0:T(8,128)}), f32[240,1024]{1,0:T(8,128)}) %all-reduce.5.cloned.1.call-update) | async-done | bytes 983056 | tf_op jit(solution)/shard_map/while/body/eval_jaxpr/psum | solution.py:31
  411.9 2.3 convolution_add_fusion.2
  414.3 2.3 fusion.32
  417.6 3.0 convolution_select_fusion.3
  420.7 187.0 %all-reduce.5.cloned.1.call-done = f32[240,1024]{1,0:T(8,128)} async-done(((f32[240,1024]{1,0:T(8,128)}), f32[240,1024]{1,0:T(8,128)}) %all-reduce.5.cloned.1.call-update) | async-done | bytes 983056 | tf_op jit(solution)/shard_map/while/body/eval_jaxpr/psum | solution.py:31
  607.7 2.3 convolution_add_fusion.2
  610.0 2.3 fusion.32
  613.3 3.0 convolution_select_fusion.3
  616.4 186.7 %all-reduce.5.cloned.1.call-done = f32[240,1024]{1,0:T(8,128)} async-done(((f32[240,1024]{1,0:T(8,128)}), f32[240,1024]{1,0:T(8,128)}) %all-reduce.5.cloned.1.call-update) | async-done | bytes 983056 | tf_op jit(solution)/shard_map/while/body/eval_jaxpr/psum | solution.py:31
  803.1 2.3 convolution_add_fusion.2
  808.7 3.0 convolution_select_fusion.3
  811.8 186.7 %all-reduce.5.cloned.1.call-done = f32[240,1024]{1,0:T(8,128)} async-done(((f32[240,1024]{1,0:T(8,128)}), f32[240,1024]{1,0:T(8,128)}) %all-reduce.5.cloned.1.call-update) | async-done | bytes 983056 | tf_op jit(solution)/shard_map/while/body/eval_jaxpr/psum | solution.py:31
  998.5 2.3 convolution_add_fusion.2
  1004.2 3.0 convolution_select_fusion.3
  1007.2 187.4 %all-reduce.5.cloned.1.call-done = f32[240,1024]{1,0:T(8,128)} async-done(((f32[240,1024]{1,0:T(8,128)}), f32[240,1024]{1,0:T(8,128)}) %all-reduce.5.cloned.1.call-update) | async-done | bytes 983056 | tf_op jit(solution)/shard_map/while/body/eval_jaxpr/psum | solution.py:31
  1194.6 2.3 convolution_add_fusion.2
  1200.3 3.0 convolution_select_fusion.3
  1203.4 187.4 %all-reduce.5.cloned.1.call-done = f32[240,1024]{1,0:T(8,128)} async-done(((f32[240,1024]{1,0:T(8,128)}), f32[240,1024]{1,0:T(8,128)}) %all-reduce.5.cloned.1.call-update) | async-done | bytes 983056 | tf_op jit(solution)/shard_map/while/body/eval_jaxpr/psum | solution.py:31
  1390.8 2.3 convolution_add_fusion.2
  1393.2 2.3 fusion.32
  1396.5 3.0 convolution_select_fusion.3
  1399.6 187.0 %all-reduce.5.cloned.1.call-done = f32[240,1024]{1,0:T(8,128)} async-done(((f32[240,1024]{1,0:T(8,128)}), f32[240,1024]{1,0:T(8,128)}) %all-reduce.5.cloned.1.call-update) | async-done | bytes 983056 | tf_op jit(solution)/shard_map/while/body/eval_jaxpr/psum | solution.py:31
  1586.6 2.3 convolution_add_fusion.2
  1593.3 8.3 all-to-all-start
  1603.0 11.3 all-to-all-done
  1615.6 43.0 %all-reduce.3.cloned.1.call-done = f32[240,256]{1,0:T(8,128)} async-done(((f32[240,256]{1,0:T(8,128)}), f32[240,256]{1,0:T(8,128)}) %all-reduce.3.cloned.1.call-update) | async-done | bytes 245776 | tf_op jit(solution)/shard_map/psum | solution.py:93
  (55 shorter events, 28.9 us)
Async XLA Ops:
  11.9 1581.4 %all-to-all-start.1 = ((s32[64,1,4]{2,1,0:T(1,128)}), s32[64,1,4]{2,1,0:T(1,128)S(1)}, u32[]{:S(2)}, u32[]{:S(2)}) async-start(s32[64,1,4]{2,1,0:T(1,128)} %bitcast.8), calls=%async_computation.1 | async-start | bytes 65536 | tf_op jit(solution)/shard_map/all_to_all | solution.py:76
  24.0 1568.2 %copy-start.2 = (f32[1,240,128]{2,1,0:T(8,128)S(1)}, f32[1,240,128]{2,1,0:T(8,128)}, u32[]{:S(2)}) copy-start(f32[1,240,128]{2,1,0:T(8,128)} %param.14) | copy-start | bytes 368644
  24.0 1634.6 %copy-start.1 = (f32[240,256]{1,0:T(8,128)S(1)}, f32[240,256]{1,0:T(8,128)}, u32[]{:S(2)}) copy-start(f32[240,256]{1,0:T(8,128)} %param.17) | copy-start | bytes 737284
  24.0 192.2 %all-reduce.5.cloned.1.call-start = ((), (), s32[]{:S(2)}) async-start(), calls=%async_computation.3 | async-start | bytes 1966080 | tf_op jit(solution)/shard_map/while/body/eval_jaxpr/psum | solution.py:31
  221.8 190.1 %all-reduce.5.cloned.1.call-start = ((), (), s32[]{:S(2)}) async-start(), calls=%async_computation.3 | async-start | bytes 1966080 | tf_op jit(solution)/shard_map/while/body/eval_jaxpr/psum | solution.py:31
  417.6 190.1 %all-reduce.5.cloned.1.call-start = ((), (), s32[]{:S(2)}) async-start(), calls=%async_computation.3 | async-start | bytes 1966080 | tf_op jit(solution)/shard_map/while/body/eval_jaxpr/psum | solution.py:31
  613.3 189.8 %all-reduce.5.cloned.1.call-start = ((), (), s32[]{:S(2)}) async-start(), calls=%async_computation.3 | async-start | bytes 1966080 | tf_op jit(solution)/shard_map/while/body/eval_jaxpr/psum | solution.py:31
  808.7 189.8 %all-reduce.5.cloned.1.call-start = ((), (), s32[]{:S(2)}) async-start(), calls=%async_computation.3 | async-start | bytes 1966080 | tf_op jit(solution)/shard_map/while/body/eval_jaxpr/psum | solution.py:31
  1004.1 190.5 %all-reduce.5.cloned.1.call-start = ((), (), s32[]{:S(2)}) async-start(), calls=%async_computation.3 | async-start | bytes 1966080 | tf_op jit(solution)/shard_map/while/body/eval_jaxpr/psum | solution.py:31
  1200.3 190.6 %all-reduce.5.cloned.1.call-start = ((), (), s32[]{:S(2)}) async-start(), calls=%async_computation.3 | async-start | bytes 1966080 | tf_op jit(solution)/shard_map/while/body/eval_jaxpr/psum | solution.py:31
  1396.4 190.2 %all-reduce.5.cloned.1.call-start = ((), (), s32[]{:S(2)}) async-start(), calls=%async_computation.3 | async-start | bytes 1966080 | tf_op jit(solution)/shard_map/while/body/eval_jaxpr/psum | solution.py:31
  1592.2 68.1 %copy-start = (f32[240,128]{1,0:T(8,128)}, f32[240,128]{1,0:T(8,128)S(1)}, u32[]{:S(2)}) copy-start(f32[240,128]{1,0:T(8,128)S(1)} %get-tuple-element.239) | copy-start | bytes 368644
  1593.3 21.0 %all-to-all-start = ((f32[64,4,240]{2,1,0:T(4,128)}), f32[64,4,240]{2,1,0:T(4,128)S(1)}, u32[]{:S(2)}, u32[]{:S(2)}) async-start(f32[64,4,240]{2,1,0:T(4,128)} %reshape.25), calls=%async_computation | async-start | bytes 524288 | tf_op jit(solution)/shard_map/all_to_all | solution.py:69
  1601.6 56.9 %all-reduce.3.cloned.1.call-start = ((), (), s32[]{:S(2)}) async-start(), calls=%async_computation.2 | async-start | bytes 491520 | tf_op jit(solution)/shard_map/psum | solution.py:93
Sparse Core Ops, SparseCore 0:
  28.2 187.9 all-reduce.4
  226.0 185.8 all-reduce.4
  421.7 185.8 all-reduce.4
  617.2 185.8 all-reduce.4
  812.6 185.8 all-reduce.4
  1008.0 186.6 all-reduce.4
  1204.5 186.3 all-reduce.4
  1400.6 185.9 all-reduce.4
Sparse Core Ops, SparseCore 1:
  1615.7 42.8 all-reduce.2
where the time goes:
time: 1670 us
  waiting for transfers between devices  1550 us (93%)
  matrix products  62.8 us (4%)
  starting transfers between devices  20.7 us (1%)
    psum x8, waiting for transfers between devices, solve_section(): solved = lax.psum(masked, ('pivot', 'rows'))  1500 us
    psum x1, waiting for transfers between devices, shards(): sibling_total = lax.psum(local_part, 'front')  43 us
  transfers between devices with their start and end apart: 11, of which 10 were waited for; matrix products, arithmetic and copies ran while one was open for 4% of the time, Pallas kernels for 0%

commit v1 on v0

--- a/solution.py
+++ b/solution.py
@@ -28,7 +28,7 @@
             residual, inv_rows, precision=highest, preferred_element_type=jnp.float32
         )
         masked = jnp.where(own_block == section_idx, partial_value, 0.0)
-        solved = lax.psum(masked, ("pivot", "rows"))
+        solved = lax.psum(lax.psum(masked, "rows"), "pivot")
         pivot_tile = lax.dynamic_slice_in_dim(factor_rows, section_idx * block_span, block_span, 1)
         update_term = lax.dot_general(
             solved, pivot_tile, contract, precision=highest, preferred_element_type=jnp.float32

time: 1670 us -> 1320 us (0.79)
  waiting for transfers between devices: 1550 us -> 1200 us
    psum x8 -> x16, waiting for transfers between devices: 1500 us -> 1140 us  [solve_section(): solved = lax.psum(lax.psum(masked, 'rows'), 'pivot')]
  transfers between devices with their start and end apart: 11 -> 19, of which waited for: 10 -> 18; matrix products, arithmetic and copies ran while one was open for 4% -> 5% of each run, Pallas kernels for 0% -> 0%
where the time goes in v1:
time: 1320 us
  waiting for transfers between devices  1200 us (91%)
  matrix products  62.8 us (5%)
  starting transfers between devices  23.6 us (2%)
  between operations  15.3 us (1%)
    psum x16, waiting for transfers between devices, solve_section(): solved = lax.psum(lax.psum(masked, 'rows'), 'pivot')  1140 us
    psum x1, waiting for transfers between devices, shards(): sibling_total = lax.psum(local_part, 'front')  43 us
  transfers between devices with their start and end apart: 19, of which 18 were waited for; matrix products, arithmetic and copies ran while one was open for 5% of the time, Pallas kernels for 0%

profile of v1, /device:TPU:2, one launch (start us, length us, event | category | flops | bytes accessed | tf_op | source)
XLA Modules:
  0.0 1317.2 jit_solution(12579974911695049596)
XLA Ops:
  11.9 12.0 all-to-all-start.1
  24.0 1215.5 %while.20 = (s32[]{:T(128)}, f32[240,128]{1,0:T(8,128)S(1)}, f32[240,128]{1,0:T(8,128)S(1)}, f32[240,128]{1,0:T(8,128)S(1)}, s32[]{:T(128)}, /*index=5*/f32[240,...) while((s32[]{:T(128)}, f32[240,128]{1,0:T(8,128)S(1)}, ...), condition=%wide.region_3.4_spmd.clone, body=%wide.region_0.3_spmd.clone.sunk | while | flops 1133475840 | bytes 17424688 | solution.py:50
  24.1 3.1 convolution_select_fusion.3
  27.2 76.9 %all-reduce.6.cloned.1.call-done = f32[240,1024]{1,0:T(8,128)} async-done(((f32[240,1024]{1,0:T(8,128)}), f32[240,1024]{1,0:T(8,128)}) %all-reduce.6.cloned.1.call-update) | async-done | bytes 983056 | tf_op jit(solution)/shard_map/while/body/eval_jaxpr/psum | solution.py:31
  104.2 66.0 %all-reduce.8.cloned.1.call-done = f32[240,1024]{1,0:T(8,128)} async-done(((f32[240,1024]{1,0:T(8,128)}), f32[240,1024]{1,0:T(8,128)}) %all-reduce.8.cloned.1.call-update) | async-done | bytes 983056 | tf_op jit(solution)/shard_map/while/body/eval_jaxpr/psum | solution.py:31
  175.9 3.0 convolution_select_fusion.3
  179.0 77.2 %all-reduce.6.cloned.1.call-done = f32[240,1024]{1,0:T(8,128)} async-done(((f32[240,1024]{1,0:T(8,128)}), f32[240,1024]{1,0:T(8,128)}) %all-reduce.6.cloned.1.call-update) | async-done | bytes 983056 | tf_op jit(solution)/shard_map/while/body/eval_jaxpr/psum | solution.py:31
  256.3 65.9 %all-reduce.8.cloned.1.call-done = f32[240,1024]{1,0:T(8,128)} async-done(((f32[240,1024]{1,0:T(8,128)}), f32[240,1024]{1,0:T(8,128)}) %all-reduce.8.cloned.1.call-update) | async-done | bytes 983056 | tf_op jit(solution)/shard_map/while/body/eval_jaxpr/psum | solution.py:31
  327.8 3.0 convolution_select_fusion.3
  330.9 77.3 %all-reduce.6.cloned.1.call-done = f32[240,1024]{1,0:T(8,128)} async-done(((f32[240,1024]{1,0:T(8,128)}), f32[240,1024]{1,0:T(8,128)}) %all-reduce.6.cloned.1.call-update) | async-done | bytes 983056 | tf_op jit(solution)/shard_map/while/body/eval_jaxpr/psum | solution.py:31
  408.2 65.9 %all-reduce.8.cloned.1.call-done = f32[240,1024]{1,0:T(8,128)} async-done(((f32[240,1024]{1,0:T(8,128)}), f32[240,1024]{1,0:T(8,128)}) %all-reduce.8.cloned.1.call-update) | async-done | bytes 983056 | tf_op jit(solution)/shard_map/while/body/eval_jaxpr/psum | solution.py:31
  479.8 3.0 convolution_select_fusion.3
  482.9 77.2 %all-reduce.6.cloned.1.call-done = f32[240,1024]{1,0:T(8,128)} async-done(((f32[240,1024]{1,0:T(8,128)}), f32[240,1024]{1,0:T(8,128)}) %all-reduce.6.cloned.1.call-update) | async-done | bytes 983056 | tf_op jit(solution)/shard_map/while/body/eval_jaxpr/psum | solution.py:31
  560.1 66.0 %all-reduce.8.cloned.1.call-done = f32[240,1024]{1,0:T(8,128)} async-done(((f32[240,1024]{1,0:T(8,128)}), f32[240,1024]{1,0:T(8,128)}) %all-reduce.8.cloned.1.call-update) | async-done | bytes 983056 | tf_op jit(solution)/shard_map/while/body/eval_jaxpr/psum | solution.py:31
  631.8 3.0 convolution_select_fusion.3
  634.9 77.3 %all-reduce.6.cloned.1.call-done = f32[240,1024]{1,0:T(8,128)} async-done(((f32[240,1024]{1,0:T(8,128)}), f32[240,1024]{1,0:T(8,128)}) %all-reduce.6.cloned.1.call-update) | async-done | bytes 983056 | tf_op jit(solution)/shard_map/while/body/eval_jaxpr/psum | solution.py:31
  712.3 65.8 %all-reduce.8.cloned.1.call-done = f32[240,1024]{1,0:T(8,128)} async-done(((f32[240,1024]{1,0:T(8,128)}), f32[240,1024]{1,0:T(8,128)}) %all-reduce.8.cloned.1.call-update) | async-done | bytes 983056 | tf_op jit(solution)/shard_map/while/body/eval_jaxpr/psum | solution.py:31
  778.1 2.3 convolution_add_fusion.2
  783.8 3.0 convolution_select_fusion.3
  786.9 77.3 %all-reduce.6.cloned.1.call-done = f32[240,1024]{1,0:T(8,128)} async-done(((f32[240,1024]{1,0:T(8,128)}), f32[240,1024]{1,0:T(8,128)}) %all-reduce.6.cloned.1.call-update) | async-done | bytes 983056 | tf_op jit(solution)/shard_map/while/body/eval_jaxpr/psum | solution.py:31
  864.2 65.9 %all-reduce.8.cloned.1.call-done = f32[240,1024]{1,0:T(8,128)} async-done(((f32[240,1024]{1,0:T(8,128)}), f32[240,1024]{1,0:T(8,128)}) %all-reduce.8.cloned.1.call-update) | async-done | bytes 983056 | tf_op jit(solution)/shard_map/while/body/eval_jaxpr/psum | solution.py:31
  930.0 2.3 convolution_add_fusion.2
  935.7 3.0 convolution_select_fusion.3
  938.8 77.3 %all-reduce.6.cloned.1.call-done = f32[240,1024]{1,0:T(8,128)} async-done(((f32[240,1024]{1,0:T(8,128)}), f32[240,1024]{1,0:T(8,128)}) %all-reduce.6.cloned.1.call-update) | async-done | bytes 983056 | tf_op jit(solution)/shard_map/while/body/eval_jaxpr/psum | solution.py:31
  1016.1 65.9 %all-reduce.8.cloned.1.call-done = f32[240,1024]{1,0:T(8,128)} async-done(((f32[240,1024]{1,0:T(8,128)}), f32[240,1024]{1,0:T(8,128)}) %all-reduce.8.cloned.1.call-update) | async-done | bytes 983056 | tf_op jit(solution)/shard_map/while/body/eval_jaxpr/psum | solution.py:31
  1087.6 3.0 convolution_select_fusion.3
  1090.7 77.3 %all-reduce.6.cloned.1.call-done = f32[240,1024]{1,0:T(8,128)} async-done(((f32[240,1024]{1,0:T(8,128)}), f32[240,1024]{1,0:T(8,128)}) %all-reduce.6.cloned.1.call-update) | async-done | bytes 983056 | tf_op jit(solution)/shard_map/while/body/eval_jaxpr/psum | solution.py:31
  1168.1 65.9 %all-reduce.8.cloned.1.call-done = f32[240,1024]{1,0:T(8,128)} async-done(((f32[240,1024]{1,0:T(8,128)}), f32[240,1024]{1,0:T(8,128)}) %all-reduce.8.cloned.1.call-update) | async-done | bytes 983056 | tf_op jit(solution)/shard_map/while/body/eval_jaxpr/psum | solution.py:31
  1233.9 2.3 convolution_add_fusion.2
  1240.6 10.8 all-to-all-start
  1252.9 11.3 all-to-all-done
  1265.4 43.0 %all-reduce.4.cloned.1.call-done = f32[240,256]{1,0:T(8,128)} async-done(((f32[240,256]{1,0:T(8,128)}), f32[240,256]{1,0:T(8,128)}) %all-reduce.4.cloned.1.call-update) | async-done | bytes 245776 | tf_op jit(solution)/shard_map/psum | solution.py:93
  (79 shorter events, 47.9 us)
Async XLA Ops:
  11.9 1228.7 %all-to-all-start.1 = ((s32[64,1,4]{2,1,0:T(1,128)}), s32[64,1,4]{2,1,0:T(1,128)S(1)}, u32[]{:S(2)}, u32[]{:S(2)}) async-start(s32[64,1,4]{2,1,0:T(1,128)} %bitcast.8), calls=%async_computation.1 | async-start | bytes 65536 | tf_op jit(solution)/shard_map/all_to_all | solution.py:76
  24.0 1215.5 %copy-start.2 = (f32[1,240,128]{2,1,0:T(8,128)S(1)}, f32[1,240,128]{2,1,0:T(8,128)}, u32[]{:S(2)}) copy-start(f32[1,240,128]{2,1,0:T(8,128)} %param.14) | copy-start | bytes 368644
  24.0 1284.4 %copy-start.1 = (f32[240,256]{1,0:T(8,128)S(1)}, f32[240,256]{1,0:T(8,128)}, u32[]{:S(2)}) copy-start(f32[240,256]{1,0:T(8,128)} %param.17) | copy-start | bytes 737284
  24.0 80.2 %all-reduce.6.cloned.1.call-start = ((), (), s32[]{:S(2)}) async-start(), calls=%async_computation.3 | async-start | bytes 1966080 | tf_op jit(solution)/shard_map/while/body/eval_jaxpr/psum | solution.py:31
  27.2 143.0 %all-reduce.8.cloned.1.call-start = ((), (), s32[]{:S(2)}) async-start(), calls=%async_computation.4 | async-start | bytes 1966080 | tf_op jit(solution)/shard_map/while/body/eval_jaxpr/psum | solution.py:31
  175.8 80.4 %all-reduce.6.cloned.1.call-start = ((), (), s32[]{:S(2)}) async-start(), calls=%async_computation.3 | async-start | bytes 1966080 | tf_op jit(solution)/shard_map/while/body/eval_jaxpr/psum | solution.py:31
  178.9 143.2 %all-reduce.8.cloned.1.call-start = ((), (), s32[]{:S(2)}) async-start(), calls=%async_computation.4 | async-start | bytes 1966080 | tf_op jit(solution)/shard_map/while/body/eval_jaxpr/psum | solution.py:31
  327.7 80.5 %all-reduce.6.cloned.1.call-start = ((), (), s32[]{:S(2)}) async-start(), calls=%async_computation.3 | async-start | bytes 1966080 | tf_op jit(solution)/shard_map/while/body/eval_jaxpr/psum | solution.py:31
  330.8 143.3 %all-reduce.8.cloned.1.call-start = ((), (), s32[]{:S(2)}) async-start(), calls=%async_computation.4 | async-start | bytes 1966080 | tf_op jit(solution)/shard_map/while/body/eval_jaxpr/psum | solution.py:31
  479.7 80.4 %all-reduce.6.cloned.1.call-start = ((), (), s32[]{:S(2)}) async-start(), calls=%async_computation.3 | async-start | bytes 1966080 | tf_op jit(solution)/shard_map/while/body/eval_jaxpr/psum | solution.py:31
  482.8 143.3 %all-reduce.8.cloned.1.call-start = ((), (), s32[]{:S(2)}) async-start(), calls=%async_computation.4 | async-start | bytes 1966080 | tf_op jit(solution)/shard_map/while/body/eval_jaxpr/psum | solution.py:31
  631.7 80.5 %all-reduce.6.cloned.1.call-start = ((), (), s32[]{:S(2)}) async-start(), calls=%async_computation.3 | async-start | bytes 1966080 | tf_op jit(solution)/shard_map/while/body/eval_jaxpr/psum | solution.py:31
  634.8 143.3 %all-reduce.8.cloned.1.call-start = ((), (), s32[]{:S(2)}) async-start(), calls=%async_computation.4 | async-start | bytes 1966080 | tf_op jit(solution)/shard_map/while/body/eval_jaxpr/psum | solution.py:31
  783.7 80.4 %all-reduce.6.cloned.1.call-start = ((), (), s32[]{:S(2)}) async-start(), calls=%async_computation.3 | async-start | bytes 1966080 | tf_op jit(solution)/shard_map/while/body/eval_jaxpr/psum | solution.py:31
  786.8 143.2 %all-reduce.8.cloned.1.call-start = ((), (), s32[]{:S(2)}) async-start(), calls=%async_computation.4 | async-start | bytes 1966080 | tf_op jit(solution)/shard_map/while/body/eval_jaxpr/psum | solution.py:31
  935.7 80.4 %all-reduce.6.cloned.1.call-start = ((), (), s32[]{:S(2)}) async-start(), calls=%async_computation.3 | async-start | bytes 1966080 | tf_op jit(solution)/shard_map/while/body/eval_jaxpr/psum | solution.py:31
  938.8 143.2 %all-reduce.8.cloned.1.call-start = ((), (), s32[]{:S(2)}) async-start(), calls=%async_computation.4 | async-start | bytes 1966080 | tf_op jit(solution)/shard_map/while/body/eval_jaxpr/psum | solution.py:31
  1087.6 80.4 %all-reduce.6.cloned.1.call-start = ((), (), s32[]{:S(2)}) async-start(), calls=%async_computation.3 | async-start | bytes 1966080 | tf_op jit(solution)/shard_map/while/body/eval_jaxpr/psum | solution.py:31
  1090.7 143.2 %all-reduce.8.cloned.1.call-start = ((), (), s32[]{:S(2)}) async-start(), calls=%async_computation.4 | async-start | bytes 1966080 | tf_op jit(solution)/shard_map/while/body/eval_jaxpr/psum | solution.py:31
  1239.5 70.6 %copy-start = (f32[240,128]{1,0:T(8,128)}, f32[240,128]{1,0:T(8,128)S(1)}, u32[]{:S(2)}) copy-start(f32[240,128]{1,0:T(8,128)S(1)} %get-tuple-element.239) | copy-start | bytes 368644
  1240.6 23.5 %all-to-all-start = ((f32[64,4,240]{2,1,0:T(4,128)}), f32[64,4,240]{2,1,0:T(4,128)S(1)}, u32[]{:S(2)}, u32[]{:S(2)}) async-start(f32[64,4,240]{2,1,0:T(4,128)} %reshape.25), calls=%async_computation | async-start | bytes 524288 | tf_op jit(solution)/shard_map/all_to_all | solution.py:69
  1251.5 56.9 %all-reduce.4.cloned.1.call-start = ((), (), s32[]{:S(2)}) async-start(), calls=%async_computation.2 | async-start | bytes 491520 | tf_op jit(solution)/shard_map/psum | solution.py:93
Sparse Core Ops, SparseCore 0:
  27.3 76.8 all-reduce.5
  106.5 63.6 all-reduce.7
  179.0 77.1 all-reduce.5
  258.4 63.6 all-reduce.7
  330.9 77.2 all-reduce.5
  410.4 63.6 all-reduce.7
  482.9 77.1 all-reduce.5
  562.5 63.6 all-reduce.7
  635.0 77.2 all-reduce.5
  714.4 63.6 all-reduce.7
  787.0 77.1 all-reduce.5
  866.4 63.6 all-reduce.7
  938.9 77.1 all-reduce.5
  1018.3 63.6 all-reduce.7
  1090.8 77.1 all-reduce.5
  1170.2 63.6 all-reduce.7
Sparse Core Ops, SparseCore 1:
  1265.5 42.9 all-reduce.3
